TPU v7x, 512 devices: a whole 4x4x16 slice. The times are simulated.
512 devices in a mesh: row: 16 (over z), col: 16 (over y, x_lo, core), depth: 2 (over x_hi).
Axes of the slice: x: 4 (x_hi: 2, x_lo: 2; x = x_hi * 2 + x_lo), y: 4, z: 16, core: 2. Of those that a mesh axis runs over, the one named last changes fastest.
Arguments:
- amplitudes: float32 [3072, 11520], P('row', ('col', 'depth')), may hold values from -6 to 6
- integrals: float32 [11520, 5760], P(('row', 'depth'), 'col'), may hold values from -0.0546875 to 0.0546875
Outputs:
- ladder: float32 [3072, 5760], P(('row', 'depth'), 'col')
All inputs are finite; a program needn't handle non-finite values.
Results may differ from a plain program's by a relative error of at most 0.00007.
Values sent between devices are 32-bit elements; how exact they have to be, the bound alone decides.
No kernel may reach another device: no remote copies, remote signals or barrier semaphores. Data moves between devices by JAX's collectives and lax.ppermute only.
A program may use at most 64 MiB of HBM per device.

v0:
```python
import jax
import jax.numpy as jnp
from jax import lax
from jax.sharding import PartitionSpec as P


def local(amplitudes, integrals):
    slab = lax.all_gather(integrals, "row", axis=0, tiled=True)
    total = jnp.dot(
        lax.all_gather(amplitudes, "col", axis=1, tiled=True),
        slab,
        precision=lax.Precision.HIGHEST,
        preferred_element_type=jnp.float32,
    )
    return lax.psum_scatter(0.5 * total, "depth", scatter_dimension=0, tiled=True)


def solution(mesh):
    placed = (P("row", ("col", "depth")), P(("row", "depth"), "col"))
    return jax.shard_map(
        local, mesh=mesh, in_specs=placed, out_specs=P(("row", "depth"), "col"), check_vma=False
    )
```

profile of v0, /device:TPU:1, one launch (start us, length us, event | category | flops | bytes accessed | tf_op | source)
XLA Modules:
  0.0 213.8 jit_solution(3228303676502207377)
XLA Ops:
  6.5 0.0 all-gather.6.cloned.1.call-start
  6.5 0.7 all-gather.6.cloned.1.call-update
  7.3 0.0 all-gather.4.cloned.1.call-start
  7.3 0.7 all-gather.4.cloned.1.call-update
  8.0 0.0 reduce-scatter.2.cloned.1.call-start
  8.1 53.4 %all-gather.6.cloned.1.call-done = f32[16,360,192]{1,2,0:T(8,128)} async-done(((f32[1,360,192]{1,2,0:T(8,128)}), f32[16,360,192]{1,2,0:T(8,128)}) %all-gather.6.cloned.1.call-update) | async-done | bytes 4423696 | tf_op jit(solution)/shard_map/all_gather | solution.py:10
  61.5 7.2 %copy.4 = f32[16,360,192]{1,0,2:T(8,128)} copy(f32[16,360,192]{1,2,0:T(8,128)} %all-gather.6.cloned.1.call-done) | data formatting | bytes 8847360 | tf_op jit(solution)/shard_map/all_gather | solution.py:10
  68.7 5.9 %reshape.1 = f32[5760,192]{0,1:T(8,128)} reshape(f32[16,360,192]{1,0,2:T(8,128)} %copy.4) | data formatting | bytes 8847360
  74.5 99.1 %all-gather.4.cloned.1.call-done = f32[5760,360]{1,0:T(8,128)} async-done(((f32[360,360]{1,0:T(8,128)}), f32[5760,360]{1,0:T(8,128)}) %all-gather.4.cloned.1.call-update) | async-done | bytes 8294416 | tf_op jit(solution)/shard_map/all_gather | solution.py:8
  173.6 11.8 %convolution_multiply_fusion = f32[192,360]{1,0:T(8,128)} fusion(f32[5760,192]{0,1:T(8,128)} %reshape.1, f32[5760,360]{1,0:T(8,128)} %all-gather.4.cloned.1.call-done), kind=kOutput, calls=%fused_computation | convolution fusion | flops 4777643520 | bytes 12994560 | tf_op jit(solution)/shard_map/dot_general | solution.py:9
  185.4 0.0 reduce-scatter.2.cloned.1.call-update
  185.5 21.8 %reduce-scatter.2.cloned.1.call-done = f32[96,360]{1,0:T(8,128)} async-done(((f32[192,360]{1,0:T(8,128)}), f32[96,360]{1,0:T(8,128)}) %reduce-scatter.2.cloned.1.call-update) | async-done | bytes 138256 | tf_op jit(solution)/shard_map/reduce_scatter | solution.py:15
Async XLA Ops:
  6.5 54.9 %all-gather.6.cloned.1.call-start = ((), (), s32[]{:S(2)}) async-start(), calls=%async_computation.3 | async-start | bytes 5013504 | tf_op jit(solution)/shard_map/all_gather | solution.py:10
  7.3 166.4 %all-gather.4.cloned.1.call-start = ((), (), s32[]{:S(2)}) async-start(), calls=%async_computation.1 | async-start | bytes 9400320 | tf_op jit(solution)/shard_map/all_gather | solution.py:8
  8.0 199.3 %reduce-scatter.2.cloned.1.call-start = ((), (), s32[]{:S(2)}) async-start(), calls=%async_computation.2 | async-start | bytes 442368 | tf_op jit(solution)/shard_map/reduce_scatter | solution.py:15
Sparse Core Ops, SparseCore 0:
  9.5 51.9 all-gather.5
  63.6 110.0 all-gather.3
  185.6 21.6 reduce-scatter.1
where the time goes:
time: 214 us
  waiting for transfers between devices  176 us (82%)
  local copies, waits for them, and re-layouts  13.1 us (6%)
  between operations  13.1 us (6%)
  matrix products  11.8 us (6%)
    all_gather x1, waiting for transfers between devices, local(): slab = lax.all_gather(integrals, 'row', axis=0, tiled=True)  99.1 us
    all_gather x1, waiting for transfers between devices, local(): lax.all_gather(amplitudes, 'col', axis=1, tiled=True)  53.4 us
    reduce_scatter x1, waiting for transfers between devices, local(): lax.psum_scatter(0.5 * total, 'depth', scatter_dimension=0, tiled=True)  21.8 us
    dot_general x1, matrix products, local(): jnp.dot(lax.all_gather(amplitudes, 'col', axis=1, tiled=True), slab, prec...  11.8 us
    all_gather x1, local copies, waits for them, and re-layouts, local(): lax.all_gather(amplitudes, 'col', axis=1, tiled=True)  7.19 us
    unnamed x1, local copies, waits for them, and re-layouts  5.87 us
  transfers between devices with their start and end apart: 3, of which 3 were waited for; matrix products, arithmetic and copies ran while one was open for 6% of the time, Pallas kernels for 0%

commit v1 on v0

--- a/solution.py
+++ b/solution.py
@@ -5,7 +5,12 @@
 
 
 def local(amplitudes, integrals):
-    slab = lax.all_gather(integrals, "row", axis=0, tiled=True)
+    ring = [integrals]
+    for hop in range(15):
+        ring.append(lax.ppermute(ring[-1], "row", [(dev, (dev + 1) % 16) for dev in range(16)]))
+    slab = jnp.roll(
+        jnp.concatenate(ring[::-1], axis=0), (lax.axis_index("row") + 1) * ring[0].shape[0], axis=0
+    )
     total = jnp.dot(
         lax.all_gather(amplitudes, "col", axis=1, tiled=True),
         slab,

time: 214 us -> 350 us (1.64)
  waiting for transfers between devices: 176 us -> 230 us
  local copies, waits for them, and re-layouts: 13.1 us -> 61.1 us
  starting transfers between devices: 0.08 us -> 31.3 us
    ppermute x0 -> x15, waiting for transfers between devices: none -> 193 us  [local(): lax.ppermute(ring[-1], 'row', [(dev, (dev + 1) % 16) for dev in range(16)])]
    all_gather x1 -> x0, waiting for transfers between devices: 99.1 us -> none  [local(): slab = lax.all_gather(integrals, 'row', axis=0, tiled=True)]
    all_gather x1, waiting for transfers between devices: 53.4 us -> 0.01 us  [local(): lax.all_gather(amplitudes, 'col', axis=1, tiled=True)]
    unnamed x1 -> x58, local copies, waits for them, and re-layouts: 5.87 us -> 53 us
    ppermute x0 -> x15, starting transfers between devices: none -> 31.2 us  [local(): lax.ppermute(ring[-1], 'row', [(dev, (dev + 1) % 16) for dev in range(16)])]
    reduce_scatter x1, waiting for transfers between devices: 21.8 us -> 36.6 us  [local(): lax.psum_scatter(0.5 * total, 'depth', scatter_dimension=0, tiled=True)]
  transfers between devices with their start and end apart: 3 -> 17, of which waited for: 3 -> 16; matrix products, arithmetic and copies ran while one was open for 6% -> 12% of each run, Pallas kernels for 0% -> 0%
where the time goes in v1:
time: 350 us; the launch traced here: 348 us
  waiting for transfers between devices  230 us (66%)
  local copies, waits for them, and re-layouts  61.1 us (17%)
  starting transfers between devices  31.3 us (9%)
  between operations  13.6 us (4%)
  matrix products  12.5 us (4%)
    ppermute x15, waiting for transfers between devices, local(): lax.ppermute(ring[-1], 'row', [(dev, (dev + 1) % 16) for dev in range(16)])  193 us
    unnamed x58, local copies, waits for them, and re-layouts  53 us
    reduce_scatter x1, waiting for transfers between devices, local(): lax.psum_scatter(0.5 * total, 'depth', scatter_dimension=0, tiled=True)  36.6 us
    ppermute x15, starting transfers between devices, local(): lax.ppermute(ring[-1], 'row', [(dev, (dev + 1) % 16) for dev in range(16)])  31.2 us
    dot_general x1, matrix products, local(): jnp.dot(lax.all_gather(amplitudes, 'col', axis=1, tiled=True), slab, prec...  12.5 us
    all_gather x1, local copies, waits for them, and re-layouts, local(): lax.all_gather(amplitudes, 'col', axis=1, tiled=True)  7.29 us
  transfers between devices with their start and end apart: 17, of which 16 were waited for; matrix products, arithmetic and copies ran while one was open for 12% of the time, Pallas kernels for 0%

profile of v1, /device:TPU:1, one launch (start us, length us, event | category | flops | bytes accessed | tf_op | source)
XLA Modules:
  0.0 348.3 jit_solution(14291873934884971619)
XLA Ops:
  6.5 4.5 %collective-permute-start = (f32[360,360]{1,0:T(8,128)}, f32[360,360]{1,0:T(8,128)S(1)}, u32[]{:S(2)}, u32[]{:S(2)}) collective-permute-start(f32[360,360]{1,0:T(8,128)} %param.3), channel_id=1, source_target_pairs={{0,32},{32,64},{64,96},{96,128},{128,160},{160,192},{192,224},{224... | collective-permute-start | bytes 1555208 | tf_op jit(solution)/shard_map/ppermute | solution.py:10
  11.0 20.0 %collective-permute-done = f32[360,360]{1,0:T(8,128)S(1)} collective-permute-done((f32[360,360]{1,0:T(8,128)}, f32[360,360]{1,0:T(8,128)S(1)}, u32[]{:S(2)}, u32[]{:S(2)}) %collective-permute-start) | collective-permute-done | bytes 518432 | tf_op jit(solution)/shard_map/ppermute | solution.py:10
  31.1 1.9 collective-permute-start.1
  33.0 14.0 %collective-permute-done.1 = f32[360,360]{1,0:T(8,128)S(1)} collective-permute-done((f32[360,360]{1,0:T(8,128)S(1)}, f32[360,360]{1,0:T(8,128)S(1)}, u32[]{:S(2)}, u32[]{:S(2)}) %collective-permute-start.1) | collective-permute-done | bytes 518432 | tf_op jit(solution)/shard_map/ppermute | solution.py:10
  47.0 1.9 collective-permute-start.2
  48.9 13.1 %collective-permute-done.2 = f32[360,360]{1,0:T(8,128)S(1)} collective-permute-done((f32[360,360]{1,0:T(8,128)S(1)}, f32[360,360]{1,0:T(8,128)S(1)}, u32[]{:S(2)}, u32[]{:S(2)}) %collective-permute-start.2) | collective-permute-done | bytes 518432 | tf_op jit(solution)/shard_map/ppermute | solution.py:10
  62.0 1.9 collective-permute-start.3
  63.9 12.1 %collective-permute-done.3 = f32[360,360]{1,0:T(8,128)S(1)} collective-permute-done((f32[360,360]{1,0:T(8,128)S(1)}, f32[360,360]{1,0:T(8,128)S(1)}, u32[]{:S(2)}, u32[]{:S(2)}) %collective-permute-start.3) | collective-permute-done | bytes 518432 | tf_op jit(solution)/shard_map/ppermute | solution.py:10
  76.0 1.9 collective-permute-start.4
  77.9 11.2 %collective-permute-done.4 = f32[360,360]{1,0:T(8,128)S(1)} collective-permute-done((f32[360,360]{1,0:T(8,128)S(1)}, f32[360,360]{1,0:T(8,128)S(1)}, u32[]{:S(2)}, u32[]{:S(2)}) %collective-permute-start.4) | collective-permute-done | bytes 518432 | tf_op jit(solution)/shard_map/ppermute | solution.py:10
  89.1 1.9 collective-permute-start.5
  91.1 10.4 %collective-permute-done.5 = f32[360,360]{1,0:T(8,128)} collective-permute-done((f32[360,360]{1,0:T(8,128)S(1)}, f32[360,360]{1,0:T(8,128)}, u32[]{:S(2)}, u32[]{:S(2)}) %collective-permute-start.5) | collective-permute-done | bytes 518432 | tf_op jit(solution)/shard_map/ppermute | solution.py:10
  101.5 1.9 collective-permute-start.6
  103.4 9.8 %collective-permute-done.6 = f32[360,360]{1,0:T(8,128)} collective-permute-done((f32[360,360]{1,0:T(8,128)}, f32[360,360]{1,0:T(8,128)}, u32[]{:S(2)}, u32[]{:S(2)}) %collective-permute-start.6) | collective-permute-done | bytes 518432 | tf_op jit(solution)/shard_map/ppermute | solution.py:10
  113.2 1.9 collective-permute-start.7
  115.1 10.2 %collective-permute-done.7 = f32[360,360]{1,0:T(8,128)S(1)} collective-permute-done((f32[360,360]{1,0:T(8,128)}, f32[360,360]{1,0:T(8,128)S(1)}, u32[]{:S(2)}, u32[]{:S(2)}) %collective-permute-start.7) | collective-permute-done | bytes 518432 | tf_op jit(solution)/shard_map/ppermute | solution.py:10
  126.1 1.9 collective-permute-start.8
  128.0 10.6 %collective-permute-done.8 = f32[360,360]{1,0:T(8,128)S(1)} collective-permute-done((f32[360,360]{1,0:T(8,128)S(1)}, f32[360,360]{1,0:T(8,128)S(1)}, u32[]{:S(2)}, u32[]{:S(2)}) %collective-permute-start.8) | collective-permute-done | bytes 518432 | tf_op jit(solution)/shard_map/ppermute | solution.py:10
  139.4 1.9 collective-permute-start.9
  141.4 11.6 %collective-permute-done.9 = f32[360,360]{1,0:T(8,128)S(1)} collective-permute-done((f32[360,360]{1,0:T(8,128)S(1)}, f32[360,360]{1,0:T(8,128)S(1)}, u32[]{:S(2)}, u32[]{:S(2)}) %collective-permute-start.9) | collective-permute-done | bytes 518432 | tf_op jit(solution)/shard_map/ppermute | solution.py:10
  153.0 0.9 copy-done.5
  153.9 1.9 collective-permute-start.10
  155.8 12.7 %collective-permute-done.10 = f32[360,360]{1,0:T(8,128)S(1)} collective-permute-done((f32[360,360]{1,0:T(8,128)S(1)}, f32[360,360]{1,0:T(8,128)S(1)}, u32[]{:S(2)}, u32[]{:S(2)}) %collective-permute-start.10) | collective-permute-done | bytes 518432 | tf_op jit(solution)/shard_map/ppermute | solution.py:10
  168.5 0.9 copy-done.7
  169.3 1.9 collective-permute-start.11
  171.3 13.8 %collective-permute-done.11 = f32[360,360]{1,0:T(8,128)S(1)} collective-permute-done((f32[360,360]{1,0:T(8,128)S(1)}, f32[360,360]{1,0:T(8,128)S(1)}, u32[]{:S(2)}, u32[]{:S(2)}) %collective-permute-start.11) | collective-permute-done | bytes 518432 | tf_op jit(solution)/shard_map/ppermute | solution.py:10
  185.8 1.9 collective-permute-start.12
  187.7 14.9 %collective-permute-done.12 = f32[360,360]{1,0:T(8,128)S(1)} collective-permute-done((f32[360,360]{1,0:T(8,128)S(1)}, f32[360,360]{1,0:T(8,128)S(1)}, u32[]{:S(2)}, u32[]{:S(2)}) %collective-permute-start.12) | collective-permute-done | bytes 518432 | tf_op jit(solution)/shard_map/ppermute | solution.py:10
  203.4 1.9 collective-permute-start.13
  205.4 15.1 %collective-permute-done.13 = f32[360,360]{1,0:T(8,128)} collective-permute-done((f32[360,360]{1,0:T(8,128)S(1)}, f32[360,360]{1,0:T(8,128)}, u32[]{:S(2)}, u32[]{:S(2)}) %collective-permute-start.13) | collective-permute-done | bytes 518432 | tf_op jit(solution)/shard_map/ppermute | solution.py:10
  220.4 1.9 collective-permute-start.14
  222.4 13.8 %collective-permute-done.14 = f32[360,360]{1,0:T(8,128)} collective-permute-done((f32[360,360]{1,0:T(8,128)}, f32[360,360]{1,0:T(8,128)}, u32[]{:S(2)}, u32[]{:S(2)}) %collective-permute-start.14) | collective-permute-done | bytes 518432 | tf_op jit(solution)/shard_map/ppermute | solution.py:10
  236.2 1.9 constant_dynamic-update-slice_fusion.31
  238.1 1.9 constant_dynamic-update-slice_fusion.30
  240.0 1.9 constant_dynamic-update-slice_fusion.29
  241.9 1.9 constant_dynamic-update-slice_fusion.28
  243.8 1.9 constant_dynamic-update-slice_fusion.27
  245.7 1.9 constant_dynamic-update-slice_fusion.26
  247.6 1.9 constant_dynamic-update-slice_fusion.25
  249.5 1.9 constant_dynamic-update-slice_fusion.24
  251.4 1.9 constant_dynamic-update-slice_fusion.23
  253.3 1.9 constant_dynamic-update-slice_fusion.22
  255.2 0.9 constant_dynamic-update-slice_fusion.21
  256.1 0.8 constant_dynamic-update-slice_fusion.20
  258.6 0.9 constant_dynamic-update-slice_fusion.17
  259.5 2.0 constant_dynamic-update-slice_fusion.16
  261.5 1.9 constant_dynamic-update-slice_fusion.15
  263.3 1.9 constant_dynamic-update-slice_fusion.14
  265.2 0.9 constant_dynamic-update-slice_fusion.13
  266.1 0.9 constant_dynamic-update-slice_fusion.12
  267.8 0.9 constant_dynamic-update-slice_fusion.10
  268.7 0.9 constant_dynamic-update-slice_fusion.9
  269.5 0.9 constant_dynamic-update-slice_fusion.8
  270.4 1.9 constant_dynamic-update-slice_fusion.7
  272.3 1.9 constant_dynamic-update-slice_fusion.6
  274.2 0.8 constant_dynamic-update-slice_fusion.5
  275.0 0.9 constant_dynamic-update-slice_fusion.4
  275.9 0.9 constant_dynamic-update-slice_fusion.3
  276.8 0.9 constant_dynamic-update-slice_fusion.2
  277.6 0.9 constant_dynamic-update-slice_fusion.1
  279.3 7.3 %copy.4 = f32[16,360,192]{1,0,2:T(8,128)} copy(f32[16,360,192]{1,2,0:T(8,128)} %all-gather.3.cloned.1.call-done) | data formatting | bytes 8847360 | tf_op jit(solution)/shard_map/all_gather | solution.py:15
  286.6 5.9 %reshape.1 = f32[5760,192]{0,1:T(8,128)} reshape(f32[16,360,192]{1,0,2:T(8,128)} %copy.4) | data formatting | bytes 8847360
  292.5 12.5 %fusion.5 = f32[192,360]{1,0:T(8,128)} fusion(f32[5760,192]{0,1:T(8,128)} %reshape.1, f32[11520,360]{1,0:T(8,128)} %constant_dynamic-update-slice_fusion, s32[]{:T(128)S(6)} %select_n.14), kind=kOutput, calls=%fused_computation.3 | convolution fusion | flops 4777643520 | bytes 13547524 | tf_op jit(solution)/shard_map/dot_general | solution.py:14
  305.0 36.6 %reduce-scatter.2.cloned.1.call-done = f32[96,360]{1,0:T(8,128)} async-done(((f32[192,360]{1,0:T(8,128)}), f32[96,360]{1,0:T(8,128)}) %reduce-scatter.2.cloned.1.call-update) | async-done | bytes 138256 | tf_op jit(solution)/shard_map/reduce_scatter | solution.py:20
  (33 shorter events, 6.7 us)
Async XLA Ops:
  6.5 271.9 %copy-start = (f32[360,360]{1,0:T(8,128)S(1)}, f32[360,360]{1,0:T(8,128)}, u32[]{:S(2)}) copy-start(f32[360,360]{1,0:T(8,128)} %param.3) | copy-start | bytes 1555204
  6.5 272.8 %all-gather.3.cloned.1.call-start = ((), (), s32[]{:S(2)}) async-start(), calls=%async_computation.2 | async-start | bytes 5013504 | tf_op jit(solution)/shard_map/all_gather | solution.py:15
  6.5 24.5 %collective-permute-start = (f32[360,360]{1,0:T(8,128)}, f32[360,360]{1,0:T(8,128)S(1)}, u32[]{:S(2)}, u32[]{:S(2)}) collective-permute-start(f32[360,360]{1,0:T(8,128)} %param.3), channel_id=1, source_target_pairs={{0,32},{32,64},{64,96},{96,128},{128,160},{160,192},{192,224},{224... | collective-permute-start | bytes 1555208 | tf_op jit(solution)/shard_map/ppermute | solution.py:10
  31.1 15.9 %collective-permute-start.1 = (f32[360,360]{1,0:T(8,128)S(1)}, f32[360,360]{1,0:T(8,128)S(1)}, u32[]{:S(2)}, u32[]{:S(2)}) collective-permute-start(f32[360,360]{1,0:T(8,128)S(1)} %collective-permute-done), channel_id=1, source_target_pairs={{0,32},{32,64},{64,96},{96,128},{128,160},{160,192},{192,224},{224... | collective-permute-start | bytes 1555208 | tf_op jit(solution)/shard_map/ppermute | solution.py:10
  47.0 15.0 %collective-permute-start.2 = (f32[360,360]{1,0:T(8,128)S(1)}, f32[360,360]{1,0:T(8,128)S(1)}, u32[]{:S(2)}, u32[]{:S(2)}) collective-permute-start(f32[360,360]{1,0:T(8,128)S(1)} %collective-permute-done.1), channel_id=1, source_target_pairs={{0,32},{32,64},{64,96},{96,128},{128,160},{160,192},{192,224},{224... | collective-permute-start | bytes 1555208 | tf_op jit(solution)/shard_map/ppermute | solution.py:10
  62.0 14.1 %collective-permute-start.3 = (f32[360,360]{1,0:T(8,128)S(1)}, f32[360,360]{1,0:T(8,128)S(1)}, u32[]{:S(2)}, u32[]{:S(2)}) collective-permute-start(f32[360,360]{1,0:T(8,128)S(1)} %collective-permute-done.2), channel_id=1, source_target_pairs={{0,32},{32,64},{64,96},{96,128},{128,160},{160,192},{192,224},{224... | collective-permute-start | bytes 1555208 | tf_op jit(solution)/shard_map/ppermute | solution.py:10
  76.0 13.1 %collective-permute-start.4 = (f32[360,360]{1,0:T(8,128)S(1)}, f32[360,360]{1,0:T(8,128)S(1)}, u32[]{:S(2)}, u32[]{:S(2)}) collective-permute-start(f32[360,360]{1,0:T(8,128)S(1)} %collective-permute-done.3), channel_id=1, source_target_pairs={{0,32},{32,64},{64,96},{96,128},{128,160},{160,192},{192,224},{224... | collective-permute-start | bytes 1555208 | tf_op jit(solution)/shard_map/ppermute | solution.py:10
  89.1 12.3 %collective-permute-start.5 = (f32[360,360]{1,0:T(8,128)S(1)}, f32[360,360]{1,0:T(8,128)}, u32[]{:S(2)}, u32[]{:S(2)}) collective-permute-start(f32[360,360]{1,0:T(8,128)S(1)} %collective-permute-done.4), channel_id=1, source_target_pairs={{0,32},{32,64},{64,96},{96,128},{128,160},{160,192},{192,224},{224... | collective-permute-start | bytes 1555208 | tf_op jit(solution)/shard_map/ppermute | solution.py:10
  101.5 11.7 %collective-permute-start.6 = (f32[360,360]{1,0:T(8,128)}, f32[360,360]{1,0:T(8,128)}, u32[]{:S(2)}, u32[]{:S(2)}) collective-permute-start(f32[360,360]{1,0:T(8,128)} %collective-permute-done.5), channel_id=1, source_target_pairs={{0,32},{32,64},{64,96},{96,128},{128,160},{160,192},{192,224},{224... | collective-permute-start | bytes 1555208 | tf_op jit(solution)/shard_map/ppermute | solution.py:10
  103.4 238.1 %reduce-scatter.2.cloned.1.call-start = ((), (), s32[]{:S(2)}) async-start(), calls=%async_computation.1 | async-start | bytes 442368 | tf_op jit(solution)/shard_map/reduce_scatter | solution.py:20
  113.2 12.1 %collective-permute-start.7 = (f32[360,360]{1,0:T(8,128)}, f32[360,360]{1,0:T(8,128)S(1)}, u32[]{:S(2)}, u32[]{:S(2)}) collective-permute-start(f32[360,360]{1,0:T(8,128)} %collective-permute-done.6), channel_id=1, source_target_pairs={{0,32},{32,64},{64,96},{96,128},{128,160},{160,192},{192,224},{224... | collective-permute-start | bytes 1555208 | tf_op jit(solution)/shard_map/ppermute | solution.py:10
  125.3 0.8 copy-start.1
  126.1 12.5 %collective-permute-start.8 = (f32[360,360]{1,0:T(8,128)S(1)}, f32[360,360]{1,0:T(8,128)S(1)}, u32[]{:S(2)}, u32[]{:S(2)}) collective-permute-start(f32[360,360]{1,0:T(8,128)S(1)} %collective-permute-done.7), channel_id=1, source_target_pairs={{0,32},{32,64},{64,96},{96,128},{128,160},{160,192},{192,224},{224... | collective-permute-start | bytes 1555208 | tf_op jit(solution)/shard_map/ppermute | solution.py:10
  138.6 0.8 copy-start.3
  139.4 13.6 %collective-permute-start.9 = (f32[360,360]{1,0:T(8,128)S(1)}, f32[360,360]{1,0:T(8,128)S(1)}, u32[]{:S(2)}, u32[]{:S(2)}) collective-permute-start(f32[360,360]{1,0:T(8,128)S(1)} %collective-permute-done.8), channel_id=1, source_target_pairs={{0,32},{32,64},{64,96},{96,128},{128,160},{160,192},{192,224},{224... | collective-permute-start | bytes 1555208 | tf_op jit(solution)/shard_map/ppermute | solution.py:10
  153.0 0.9 copy-start.5
  153.9 14.6 %collective-permute-start.10 = (f32[360,360]{1,0:T(8,128)S(1)}, f32[360,360]{1,0:T(8,128)S(1)}, u32[]{:S(2)}, u32[]{:S(2)}) collective-permute-start(f32[360,360]{1,0:T(8,128)S(1)} %collective-permute-done.9), channel_id=1, source_target_pairs={{0,32},{32,64},{64,96},{96,128},{128,160},{160,192},{192,224},{224... | collective-permute-start | bytes 1555208 | tf_op jit(solution)/shard_map/ppermute | solution.py:10
  168.5 0.9 copy-start.7
  169.3 15.7 %collective-permute-start.11 = (f32[360,360]{1,0:T(8,128)S(1)}, f32[360,360]{1,0:T(8,128)S(1)}, u32[]{:S(2)}, u32[]{:S(2)}) collective-permute-start(f32[360,360]{1,0:T(8,128)S(1)} %collective-permute-done.10), channel_id=1, source_target_pairs={{0,32},{32,64},{64,96},{96,128},{128,160},{160,192},{192,224},{224... | collective-permute-start | bytes 1555208 | tf_op jit(solution)/shard_map/ppermute | solution.py:10
  185.0 0.8 copy-start.9
  185.8 16.8 %collective-permute-start.12 = (f32[360,360]{1,0:T(8,128)S(1)}, f32[360,360]{1,0:T(8,128)S(1)}, u32[]{:S(2)}, u32[]{:S(2)}) collective-permute-start(f32[360,360]{1,0:T(8,128)S(1)} %collective-permute-done.11), channel_id=1, source_target_pairs={{0,32},{32,64},{64,96},{96,128},{128,160},{160,192},{192,224},{224... | collective-permute-start | bytes 1555208 | tf_op jit(solution)/shard_map/ppermute | solution.py:10
  202.7 0.8 copy-start.11
  203.4 17.0 %collective-permute-start.13 = (f32[360,360]{1,0:T(8,128)S(1)}, f32[360,360]{1,0:T(8,128)}, u32[]{:S(2)}, u32[]{:S(2)}) collective-permute-start(f32[360,360]{1,0:T(8,128)S(1)} %collective-permute-done.12), channel_id=1, source_target_pairs={{0,32},{32,64},{64,96},{96,128},{128,160},{160,192},{192,224},{224... | collective-permute-start | bytes 1555208 | tf_op jit(solution)/shard_map/ppermute | solution.py:10
  220.4 15.8 %collective-permute-start.14 = (f32[360,360]{1,0:T(8,128)}, f32[360,360]{1,0:T(8,128)}, u32[]{:S(2)}, u32[]{:S(2)}) collective-permute-start(f32[360,360]{1,0:T(8,128)} %collective-permute-done.13), channel_id=1, source_target_pairs={{0,32},{32,64},{64,96},{96,128},{128,160},{160,192},{192,224},{224... | collective-permute-start | bytes 1555208 | tf_op jit(solution)/shard_map/ppermute | solution.py:10
  222.4 42.8 %copy-start.12 = (f32[360,360]{1,0:T(8,128)S(1)}, f32[360,360]{1,0:T(8,128)}, u32[]{:S(2)}) copy-start(f32[360,360]{1,0:T(8,128)} %copy-done.11) | copy-start | bytes 1555204
  222.4 43.7 %copy-start.10 = (f32[360,360]{1,0:T(8,128)S(1)}, f32[360,360]{1,0:T(8,128)}, u32[]{:S(2)}) copy-start(f32[360,360]{1,0:T(8,128)} %copy-done.9) | copy-start | bytes 1555204
  222.4 44.6 %copy-start.8 = (f32[360,360]{1,0:T(8,128)S(1)}, f32[360,360]{1,0:T(8,128)}, u32[]{:S(2)}) copy-start(f32[360,360]{1,0:T(8,128)} %copy-done.7) | copy-start | bytes 1555204
  222.4 45.4 %copy-start.6 = (f32[360,360]{1,0:T(8,128)S(1)}, f32[360,360]{1,0:T(8,128)}, u32[]{:S(2)}) copy-start(f32[360,360]{1,0:T(8,128)} %copy-done.5) | copy-start | bytes 1555204
  222.4 46.2 %copy-start.4 = (f32[360,360]{1,0:T(8,128)S(1)}, f32[360,360]{1,0:T(8,128)}, u32[]{:S(2)}) copy-start(f32[360,360]{1,0:T(8,128)} %copy-done.3) | copy-start | bytes 1555204
  222.4 47.1 %copy-start.2 = (f32[360,360]{1,0:T(8,128)S(1)}, f32[360,360]{1,0:T(8,128)}, u32[]{:S(2)}) copy-start(f32[360,360]{1,0:T(8,128)} %copy-done.1) | copy-start | bytes 1555204
Sparse Core Ops, SparseCore 0:
  103.5 48.6 all-gather.2
  305.1 36.3 reduce-scatter.1
